TPU v7x, 128 devices: a whole 4x4x4 slice. The times are simulated.
128 devices in a mesh: slab: 8 (over y_hi, x), line: 16 (over z, y_lo, core).
Axes of the slice: x: 4, y: 4 (y_hi: 2, y_lo: 2; y = y_hi * 2 + y_lo), z: 4, core: 2. Of those that a mesh axis runs over, the one named last changes fastest.
Arguments:
- estimate: float32 [256, 256, 256], P('slab', 'line'), may hold values from -6 to 6
- support_lo: int32 [256, 256], P('slab', 'line'), may hold values from 0 to 63
- support_hi: int32 [256, 256], P('slab', 'line'), may hold values from 193 to 256
- measured: bfloat16 [2, 2, 512, 512, 2, 128], P(None, None, None, ('slab', 'line')), may hold values from -3 to 3
- blocks: int32 [512, 2, 2], replicated, may hold values from 0 to 3, all different within a row
- wedge: int32 [2], replicated, may hold values from 0 to 511
Outputs:
- updated: float32 [256, 256, 256], P('slab', 'line')
Inputs may be any that keep to these rules, and one draw needn't show every extreme that they name: The 2 entries of blocks for one plane frequency and group are distinct.
All inputs are finite; a program needn't handle non-finite values.
Results may differ from a plain program's by a relative error of at most 0.0071.
Values may be sent and summed in bfloat16 or wider, within the bound.
A program may use at most 128 MiB of HBM per device.

v0:
```python
import math
import jax
import jax.numpy as jnp
from jax import lax
from jax.sharding import PartitionSpec as P

N = 512


def phase_table(left_int, right_int, period):
    product = jnp.mod(left_int * right_int, period)
    angle = product.astype(jnp.float32) * (2.0 * math.pi / period)
    factor = 1.0 / math.sqrt(N)
    return (
        (jnp.cos(angle) * factor).astype(jnp.bfloat16),
        (jnp.sin(angle) * factor).astype(jnp.bfloat16),
    )


def contract(form, left_op, right_op):
    return jnp.einsum(form, left_op, right_op, preferred_element_type=jnp.float32)


def shards(estimate, support_lo, support_hi, measured, blocks, wedge):
    slab_count = lax.axis_size("slab")
    line_count = lax.axis_size("line")
    slab_index = lax.axis_index("slab")
    line_index = lax.axis_index("line")
    plane_rows, row_count, obj_len = estimate.shape
    half_freq = N // 2
    per_line = N // line_count
    per_device = per_line // slab_count
    per_slab = N // slab_count
    cell_coord = jnp.arange(obj_len, dtype=jnp.int32) - obj_len // 2
    local_order = jnp.arange(per_line, dtype=jnp.int32)
    plane_freq = (
        local_order // per_device * per_slab + line_index * per_device + local_order % per_device
    )
    plane_cos, slice_sine_table = phase_table(
        (plane_freq - half_freq)[:, None], cell_coord[None, :], N
    )
    cells = estimate.astype(jnp.bfloat16)
    zero_block = jnp.zeros((plane_rows, per_line, obj_len), jnp.float32)
    piece = lax.all_gather(cells, "line", axis=1, tiled=True)
    imag_a = zero_block
    real_a = contract("kx,zxy->zky", plane_cos, piece)
    imag_a = imag_a - contract("kx,zxy->zky", slice_sine_table, piece)
    real_b = contract("ky,zxy->zkx", plane_cos, piece)
    imag_b = -contract("ky,zxy->zkx", slice_sine_table, piece)
    real_a, imag_a, real_b, imag_b = (real_a, imag_a, real_b, imag_b)
    spectrum = jnp.stack([jnp.stack([real_a, imag_a]), jnp.stack([real_b, imag_b])]).astype(
        jnp.bfloat16
    )
    gathered = lax.all_to_all(spectrum, "slab", split_axis=3, concat_axis=2, tiled=True)
    own_freq = (
        slab_index * per_slab + line_index * per_device + jnp.arange(per_device, dtype=jnp.int32)
    )
    all_freq = jnp.arange(N, dtype=jnp.int32) - half_freq
    dz_cos, dz_sin = phase_table(all_freq[:, None], cell_coord[None, :], N)
    pen_re = (
        contract("az,gzkc->gakc", dz_cos, gathered[:, 0])
        + contract("az,gzkc->gakc", dz_sin, gathered[:, 1])
    ).astype(jnp.bfloat16)
    pen_im = (
        contract("az,gzkc->gakc", dz_cos, gathered[:, 1])
        - contract("az,gzkc->gakc", dz_sin, gathered[:, 0])
    ).astype(jnp.bfloat16)
    frac_cos, frac_sin = phase_table(
        (2 * (own_freq - half_freq))[:, None, None] * all_freq[None, :, None],
        cell_coord[None, None, :],
        N * N,
    )
    polar_re = contract("klc,gakc->gakl", frac_cos, pen_re) + contract(
        "klc,gakc->gakl", frac_sin, pen_im
    )
    polar_im = contract("klc,gakc->gakl", frac_cos, pen_im) - contract(
        "klc,gakc->gakl", frac_sin, pen_re
    )
    block_len = measured.shape[-1]
    nblocks = N // block_len
    block_ids = jnp.arange(nblocks, dtype=jnp.int32)
    indicator_matrix = (blocks[:, :, :, None] == block_ids).astype(jnp.bfloat16)
    covered = jnp.any(blocks[:, :, :, None] == block_ids, axis=2)
    overwritten_result = contract("voef,ozvnei->ozvnfi", indicator_matrix, measured)
    low_end = jnp.minimum(wedge[0], wedge[1])
    high_end = jnp.maximum(wedge[0], wedge[1])
    line_pos = jnp.arange(N, dtype=jnp.int32)
    excluded = ((line_pos >= low_end) & (line_pos < high_end)).reshape(nblocks, block_len)
    usable = (
        jnp.transpose(covered, (1, 0, 2))[:, :, None, :, None] & (~excluded)[None, None, None, :, :]
    )
    kweight = ((jnp.abs(own_freq - half_freq).astype(jnp.float32) + 1.0) / half_freq)[
        None, None, :, None, None
    ]
    shape_five = (2, N, per_device, nblocks, block_len)
    weighted_re = (
        (jnp.where(usable, overwritten_result[:, 0], polar_re.reshape(shape_five)) * kweight)
        .reshape(2, N, per_device, N)
        .astype(jnp.bfloat16)
    )
    weighted_im = (
        (jnp.where(usable, overwritten_result[:, 1], polar_im.reshape(shape_five)) * kweight)
        .reshape(2, N, per_device, N)
        .astype(jnp.bfloat16)
    )
    adj_re = (
        contract("klc,gakl->gakc", frac_cos, weighted_re)
        - contract("klc,gakl->gakc", frac_sin, weighted_im)
    ).astype(jnp.bfloat16)
    adj_im = (
        contract("klc,gakl->gakc", frac_cos, weighted_im)
        + contract("klc,gakl->gakc", frac_sin, weighted_re)
    ).astype(jnp.bfloat16)
    plan_re = (
        contract("az,gakc->gzkc", dz_cos, adj_re) - contract("az,gakc->gzkc", dz_sin, adj_im)
    ).astype(jnp.bfloat16)
    plan_im = (
        contract("az,gakc->gzkc", dz_cos, adj_im) + contract("az,gakc->gzkc", dz_sin, adj_re)
    ).astype(jnp.bfloat16)
    returned = lax.all_to_all(
        jnp.stack([plan_re, plan_im], axis=1), "slab", split_axis=2, concat_axis=3, tiled=True
    )
    partial_image = contract("kx,zky->zxy", plane_cos, returned[0, 0]) - contract(
        "kx,zky->zxy", slice_sine_table, returned[0, 1]
    )
    partial_image = (
        partial_image
        + contract("ky,zkx->zxy", plane_cos, returned[1, 0])
        - contract("ky,zkx->zxy", slice_sine_table, returned[1, 1])
    )
    summed = lax.psum_scatter(partial_image, "line", scatter_dimension=1, tiled=True)
    ycoord = jnp.arange(obj_len, dtype=jnp.int32)
    inside = (ycoord[None, None, :] >= support_lo[:, :, None]) & (
        ycoord[None, None, :] < support_hi[:, :, None]
    )
    return jnp.where(inside & (summed > 0.0), summed, jnp.float32(0.0))


def solution(mesh):
    in_specs = (
        P("slab", "line", None),
        P("slab", "line"),
        P("slab", "line"),
        P(None, None, None, ("slab", "line"), None, None),
        P(),
        P(),
    )
    out_specs = P("slab", "line", None)
    return jax.shard_map(shards, mesh=mesh, in_specs=in_specs, out_specs=out_specs, check_vma=False)
```

profile of v0, /device:TPU:0, one launch (start us, length us, event | category | flops | bytes accessed | tf_op | source)
XLA Modules:
  0.0 397.7 jit_solution(11599687042185202227)
XLA Ops:
  6.5 0.0 all-gather.2.cloned.1.call-start
  6.5 1.8 convert_element_type.109
  8.3 0.0 all-gather.2.cloned.1.call-update
  8.3 1.4 fusion.223
  12.2 0.9 copy.70
  13.2 12.0 %convolution_bitcast_fusion = f32[2,2,512,4,4,128]{5,4,3,1,2,0:T(4,128)} fusion(bf16[2,2,512,4,2,128]{5,4,3,2,1,0:T(2,128)(2,1)} %param.9, s32[512,2,2]{2,0,1:T(8,128)S(1)} %copy.70), kind=kOutput, calls=%fused_computation | convolution fusion | flops 16785408 | bytes 20979712 | tf_op jit(solution)/shard_map/voef,ozvnei->ozvnfi/dot_general | solution.py:21
  25.2 23.5 %all-gather.2.cloned.1.call-done = bf16[32,256,256]{2,1,0:T(8,128)(2,1)} async-done(((bf16[32,16,256]{2,1,0:T(8,128)(2,1)}), bf16[32,256,256]{2,1,0:T(8,128)(2,1)}) %all-gather.2.cloned.1.call-update) | async-done | bytes 4194320 | tf_op jit(solution)/shard_map/all_gather | solution.py:44
  48.8 3.3 fusion.43
  52.1 0.1 copy-done
  52.2 1.0 fusion.40
  53.2 1.4 fusion.42
  54.6 1.4 fusion.41
  56.0 0.2 maximum_bitcast_fusion
  56.2 0.2 pad_maximum_fusion
  56.4 2.5 copy.72
  58.9 6.5 %all-to-all-start = ((bf16[2,2,32,32,256]{4,2,1,0,3:T(8,128)(2,1)}), bf16[2,2,32,32,256]{4,2,1,0,3:T(8,128)(2,1)S(1)}, u32[]{:S(2)}, u32[]{:S(2)}) async-start(bf16[2,2,32,32,256]{4,2,1,0,3:T(8,128)(2,1)} %copy.72), calls=%async_computation | async-start | bytes 4194304 | tf_op jit(solution)/shard_map/all_to_all | solution.py:54
  65.4 0.5 reduce-scatter.2.cloned.1.call-start
  65.9 12.3 %fusion.222 = (f32[2,1,512,4,4,128]{5,4,3,1,2,0:T(4,128)}, f32[2,1,512,4,4,128]{5,4,3,1,2,0:T(4,128)}) fusion(f32[2,2,512,4,4,128]{5,4,3,1,2,0:T(4,128)} %convolution_bitcast_fusion), kind=kLoop, calls=%fused_computation.250 | loop fusion | bytes 33554432 | tf_op jit(solution)/shard_map/slice | solution.py:97
  78.2 10.6 %squeeze.33 = f32[2,512,4,512]{3,2,1,0:T(4,128)} reshape(f32[2,1,512,4,4,128]{5,4,3,1,2,0:T(4,128)} %get-tuple-element.6) | data formatting | bytes 16777216 | tf_op jit(solution)/shard_map/squeeze | solution.py:102
  88.8 5.8 %fusion.56 = pred[512,2,4]{2,0,1:T(8,128)(4,1)S(1)} fusion(s32[512,2,2]{2,0,1:T(8,128)S(1)} %copy.70), kind=kLoop, calls=%fused_computation.68 | loop fusion | flops 12288 | bytes 12288 | tf_op jit(solution)/shard_map/reduce_or | solution.py:83
  94.7 3.5 and.95
  98.1 0.5 and.96
  98.6 10.7 %squeeze.30 = f32[2,512,4,512]{3,2,1,0:T(4,128)} reshape(f32[2,1,512,4,4,128]{5,4,3,1,2,0:T(4,128)} %get-tuple-element.5) | data formatting | bytes 16777216 | tf_op jit(solution)/shard_map/squeeze | solution.py:97
  109.3 0.1 broadcast_multiply_fusion
  109.4 0.3 broadcast_and_fusion
  109.7 0.0 all-to-all-done
  109.7 0.2 copy.74
  109.9 2.7 fusion.58
  112.5 2.7 fusion.57
  115.2 3.1 fusion.25
  118.3 3.3 fusion.24
  121.6 0.0 slice-start
  121.6 11.8 %fusion.18 = f32[4,2,512,512]{3,2,1,0:T(8,128)} fusion(bf16[2,512,4,256]{1,3,2,0:T(8,128)(2,1)S(1)} %fusion.25, s32[256]{0:T(256)S(1)} %iota_add_fusion.1, s32[4,512]{1,0:T(4,128)S(1)} %broadcast_multiply_fusion), kind=kOutput, calls=%fused_computation.37 | convolution fusion | flops 1082130432 | bytes 10494976 | tf_op jit(solution)/shard_map/klc,gakc->gakl/dot_general | solution.py:21
  133.4 8.9 %fusion.22 = f32[4,2,512,512]{3,2,1,0:T(8,128)S(1)} fusion(bf16[2,512,4,256]{1,3,2,0:T(8,128)(2,1)S(1)} %fusion.24, s32[256]{0:T(256)S(1)} %iota_add_fusion.1, s32[4,512]{1,0:T(4,128)S(1)} %broadcast_multiply_fusion), kind=kOutput, calls=%fused_computation.41 | convolution fusion | flops 1082130432 | bytes 10494976 | tf_op jit(solution)/shard_map/klc,gakc->gakl/dot_general | solution.py:21
  142.3 0.0 slice-done
  142.3 0.0 slice-done.1
  142.4 0.0 slice-start.3
  142.4 15.3 %fusion.2 = bf16[2,512,4,512]{3,1,0,2:T(8,128)(2,1)} fusion(f32[2,512,4,512]{3,2,1,0:T(4,128)S(1)} %bitcast.156, f32[4,2,512,512]{3,2,1,0:T(8,128)} %fusion.18, f32[4]{0:T(128)S(1)} %add_multiply_fusion, pred[2,512,512]{2,1,0:T(8,128)(4,1)S(1)} %broadcast_and_fusion, bf16[2,512,4,256]{1,3,2,0:T(8,128)(2,1)S(1)} %fusion.24, s32[256]{0:T(256)S(1)} %iota_add_fusion.1, ...), kind=kOutput, calls=%fused_computation.5 | convolution fusion | flops 1090519040 | bytes 23602192 | tf_op jit(solution)/shard_map/klc,gakc->gakl/dot_general | solution.py:21
  157.7 12.2 %fusion.50 = f32[4,2,512,256]{3,2,1,0:T(8,128)} fusion(bf16[2,512,4,512]{3,1,0,2:T(8,128)(2,1)} %fusion.2, s32[256]{0:T(256)S(1)} %iota_add_fusion.1, s32[4,512]{1,0:T(4,128)S(1)} %broadcast_multiply_fusion), kind=kOutput, calls=%fused_computation.65 | convolution fusion | flops 1082130432 | bytes 8397824 | tf_op jit(solution)/shard_map/klc,gakl->gakc/dot_general | solution.py:21
  169.9 12.5 %fusion.4 = bf16[2,512,4,512]{3,1,0,2:T(8,128)(2,1)S(1)} fusion(f32[2,512,4,512]{3,2,1,0:T(4,128)S(1)} %bitcast.158, f32[4,2,512,512]{3,2,1,0:T(8,128)S(1)} %fusion.22, f32[4]{0:T(128)S(1)} %add_multiply_fusion, pred[2,512,512]{2,1,0:T(8,128)(4,1)S(1)} %broadcast_and_fusion, bf16[2,512,4,256]{1,3,2,0:T(8,128)(2,1)S(1)} %fusion.25, ...), kind=kOutput, calls=%fused_computation.8 | convolution fusion | flops 1090519040 | bytes 23602192 | tf_op jit(solution)/shard_map/klc,gakc->gakl/dot_general | solution.py:21
  182.5 8.5 %fusion.53 = f32[4,2,512,256]{3,2,1,0:T(8,128)S(1)} fusion(bf16[2,512,4,512]{3,1,0,2:T(8,128)(2,1)S(1)} %fusion.4, s32[256]{0:T(256)S(1)} %iota_add_fusion.1, s32[4,512]{1,0:T(4,128)S(1)} %broadcast_multiply_fusion), kind=kOutput, calls=%fused_computation.66 | convolution fusion | flops 1082130432 | bytes 8397824 | tf_op jit(solution)/shard_map/klc,gakl->gakc/dot_general | solution.py:21
  191.0 0.0 copy-done.4
  191.0 9.8 %fusion.27 = bf16[2,512,4,256]{3,1,0,2:T(8,128)(2,1)S(1)} fusion(f32[4,2,512,256]{3,2,1,0:T(8,128)S(1)} %copy-done.4, bf16[2,512,4,512]{3,1,0,2:T(8,128)(2,1)S(1)} %fusion.4, s32[256]{0:T(256)S(1)} %iota_add_fusion.1, s32[4,512]{1,0:T(4,128)S(1)} %broadcast_multiply_fusion), kind=kOutput, calls=%fused_computation.46 | convolution fusion | flops 1084227584 | bytes 10494976 | tf_op jit(solution)/shard_map/klc,gakl->gakc/dot_general | solution.py:21
  200.8 2.7 fusion.10
  203.5 2.7 fusion.12
  206.2 9.9 %fusion.26 = bf16[2,512,4,256]{3,1,0,2:T(8,128)(2,1)S(1)} fusion(f32[4,2,512,256]{3,2,1,0:T(8,128)S(1)} %fusion.53, bf16[2,512,4,512]{3,1,0,2:T(8,128)(2,1)S(1)} %copy-done.3, s32[256]{0:T(256)S(1)} %iota_add_fusion.1, s32[4,512]{1,0:T(4,128)S(1)} %broadcast_multiply_fusion), kind=kOutput, calls=%fused_computation.45 | convolution fusion | flops 1084227584 | bytes 10494976 | tf_op jit(solution)/shard_map/klc,gakl->gakc/dot_general | solution.py:21
  216.2 2.7 fusion.35
  218.9 2.7 fusion.32
  221.6 0.2 pad_maximum_fusion.1
  221.8 3.1 copy.87
  224.9 35.7 %all_to_all.36 = bf16[2,2,256,4,256]{4,3,0,1,2:T(4,128)(2,1)S(1)} all-to-all(bf16[2,2,256,4,256]{4,3,0,1,2:T(4,128)(2,1)} %copy.87), channel_id=1, replica_groups=mesh['slab'=8,'line'=16] {'slab'}, dimensions={2} | all-to-all | bytes 4194304 | tf_op jit(solution)/shard_map/all_to_all | solution.py:120
  260.7 0.7 copy.88
  261.4 3.0 copy.89
  264.4 2.5 all_to_all.33
  266.9 1.5 fusion.62
  268.4 1.4 fusion.64
  269.8 4.7 %fusion.63 = f32[32,256,256]{2,1,0:T(8,128)} fusion(bf16[2,2,32,32,256]{4,3,2,1,0:T(8,128)(2,1)S(1)} %all_to_all.33, s32[256]{0:T(256)S(1)} %iota_add_fusion.1, s32[32]{0:T(128)S(1)} %fusion.98), kind=kOutput, calls=%fused_computation.84 | convolution fusion | flops 134348800 | bytes 8914432 | tf_op jit(solution)/shard_map/kx,zky->zxy/dot_general | solution.py:21
  274.5 8.9 %fusion = f32[32,256,256]{1,2,0:T(8,128)} fusion(f32[32,256,256]{1,2,0:T(8,128)S(1)} %fusion.62, f32[32,256,256]{2,1,0:T(8,128)S(1)} %fusion.64, f32[32,256,256]{2,1,0:T(8,128)} %fusion.63, bf16[2,2,32,32,256]{4,3,2,1,0:T(8,128)(2,1)S(1)} %all_to_all.33, s32[256]{0:T(256)S(1)} %iota_add_fusion.1, s32[32]{0:T(128)S(1)} %fusion.98), kind=kOutput, calls=%fused_computation.2 | convolution fusion | flops 140640256 | bytes 34080256 | tf_op jit(solution)/shard_map/ky,zkx->zxy/dot_general | solution.py:21
  283.4 10.3 %copy.92 = f32[32,256,256]{2,0,1:T(8,128)} copy(f32[32,256,256]{1,2,0:T(8,128)} %fusion) | data formatting | bytes 16777216 | tf_op jit(solution)/shard_map/sub | solution.py:127
  293.7 0.0 reduce-scatter.2.cloned.1.call-update
  293.8 94.5 %reduce-scatter.2.cloned.1.call-done = f32[32,16,256]{2,0,1:T(8,128)} async-done(((f32[32,256,256]{2,0,1:T(8,128)}), f32[32,16,256]{2,0,1:T(8,128)}) %reduce-scatter.2.cloned.1.call-update) | async-done | bytes 524304 | tf_op jit(solution)/shard_map/reduce_scatter | solution.py:131
  388.2 0.0 copy-done.1
  388.2 1.2 fusion.68
  389.5 1.1 copy.93
  (19 shorter events, 0.1 us)
Async XLA Ops:
  6.5 42.2 %all-gather.2.cloned.1.call-start = ((), (), s32[]{:S(2)}) async-start(), calls=%async_computation.3 | async-start | bytes 4456448 | tf_op jit(solution)/shard_map/all_gather | solution.py:44
  48.8 3.4 copy-start
  58.9 50.8 %all-to-all-start = ((bf16[2,2,32,32,256]{4,2,1,0,3:T(8,128)(2,1)}), bf16[2,2,32,32,256]{4,2,1,0,3:T(8,128)(2,1)S(1)}, u32[]{:S(2)}, u32[]{:S(2)}) async-start(bf16[2,2,32,32,256]{4,2,1,0,3:T(8,128)(2,1)} %copy.72), calls=%async_computation | async-start | bytes 4194304 | tf_op jit(solution)/shard_map/all_to_all | solution.py:54
  65.4 322.8 %reduce-scatter.2.cloned.1.call-start = ((), (), s32[]{:S(2)}) async-start(), calls=%async_computation.4 | async-start | bytes 8912896 | tf_op jit(solution)/shard_map/reduce_scatter | solution.py:131
  121.6 20.7 %slice-start = ((s8[8388608]{0:T(1024)(128)(4,1)}), s8[4194304]{0:T(1024)(128)(4,1)S(1)}, s32[]{:S(2)}) async-start(s8[8388608]{0:T(1024)(128)(4,1)} %bitcast.155), calls=%async_computation.5 | async-start | bytes 8388608
  133.4 8.9 %slice-start.1 = ((s8[8388608]{0:T(1024)(128)(4,1)}), s8[4194304]{0:T(1024)(128)(4,1)S(1)}, s32[]{:S(2)}) async-start(s8[8388608]{0:T(1024)(128)(4,1)} %bitcast.155), calls=%async_computation.6 | async-start | bytes 8388608
  133.4 36.5 %slice-start.2 = ((s8[8388608]{0:T(1024)(128)(4,1)}), s8[4194304]{0:T(1024)(128)(4,1)S(1)}, s32[]{:S(2)}) async-start(s8[8388608]{0:T(1024)(128)(4,1)} %bitcast.157), calls=%async_computation.7 | async-start | bytes 8388608
  142.4 27.6 %slice-start.3 = ((s8[8388608]{0:T(1024)(128)(4,1)}), s8[4194304]{0:T(1024)(128)(4,1)S(1)}, s32[]{:S(2)}) async-start(s8[8388608]{0:T(1024)(128)(4,1)} %bitcast.157), calls=%async_computation.8 | async-start | bytes 8388608
  182.5 8.5 %copy-start.4 = (f32[4,2,512,256]{3,2,1,0:T(8,128)S(1)}, f32[4,2,512,256]{3,2,1,0:T(8,128)}, u32[]{:S(2)}) copy-start(f32[4,2,512,256]{3,2,1,0:T(8,128)} %fusion.50) | copy-start | bytes 12582916
  203.5 2.7 copy-start.3
  293.7 94.5 %copy-start.1 = (s32[32,16]{0,1:T(8,128)S(1)}, s32[32,16]{0,1:T(8,128)}, u32[]{:S(2)}) copy-start(s32[32,16]{0,1:T(8,128)} %param.8) | copy-start | bytes 6148
  293.7 94.5 %copy-start.2 = (s32[32,16]{0,1:T(8,128)S(1)}, s32[32,16]{0,1:T(8,128)}, u32[]{:S(2)}) copy-start(s32[32,16]{0,1:T(8,128)} %param.7) | copy-start | bytes 6148
Sparse Core Ops, SparseCore 0:
  9.0 39.7 all-gather.1
  293.9 94.2 reduce-scatter.1
where the time goes:
time: 404 us; the launch traced here: 398 us
  matrix products  147 us (36%)
  waiting for transfers between devices  118 us (29%)
  local copies, waits for them, and re-layouts  63.4 us (16%)
  blocking collectives  35.7 us (9%)
  between operations  16.5 us (4%)
  other arithmetic  9.83 us (2%)
  starting transfers between devices  7.02 us (2%)
    dot_general x25, matrix products, contract(): jnp.einsum(form, left_op, right_op, preferred_element_type=jnp.float32)  147 us
    reduce_scatter x1, waiting for transfers between devices, shards(): lax.psum_scatter(partial_image, 'line', scatter_dimension=1, tiled=True)  94.5 us
    all_to_all x1, blocking collectives, shards(): lax.all_to_all(jnp.stack([plan_re, plan_im], axis=1), 'slab', split_axis=...  35.7 us
    all_gather x1, waiting for transfers between devices, shards(): piece = lax.all_gather(cells, 'line', axis=1, tiled=True)  23.5 us
    slice x1, local copies, waits for them, and re-layouts, shards(): overwritten_result[:, 0]  12.3 us
    squeeze x1, local copies, waits for them, and re-layouts, shards(): overwritten_result[:, 0]  10.7 us
    squeeze x1, local copies, waits for them, and re-layouts, shards(): overwritten_result[:, 1]  10.6 us
    sub x1, local copies, waits for them, and re-layouts, shards(): partial_image + contract('ky,zkx->zxy', plane_cos, returned[1, 0])  10.3 us
  transfers between devices with their start and end apart: 3, of which 2 were waited for; matrix products, arithmetic and copies ran while one was open for 15% of the time, Pallas kernels for 0%

commit v1 on v0

--- a/solution.py
+++ b/solution.py
@@ -41,7 +41,9 @@
     )
     cells = estimate.astype(jnp.bfloat16)
     zero_block = jnp.zeros((plane_rows, per_line, obj_len), jnp.float32)
-    piece = lax.all_gather(cells, "line", axis=1, tiled=True)
+    piece = jnp.concatenate(
+        lax.all_to_all(jnp.stack([cells] * lax.axis_size("line")), "line", 0, 0), axis=1
+    )
     imag_a = zero_block
     real_a = contract("kx,zxy->zky", plane_cos, piece)
     imag_a = imag_a - contract("kx,zxy->zky", slice_sine_table, piece)

time: 404 us -> 422 us (1.045)
  waiting for transfers between devices: 118 us -> 129 us
  starting transfers between devices: 7.02 us -> 13.9 us
    all_to_all x0 -> x1, waiting for transfers between devices: none -> 34.9 us  [shards(): lax.all_to_all(jnp.stack([cells] * lax.axis_size('line')), 'line', 0, 0)]
    all_gather x1 -> x0, waiting for transfers between devices: 23.5 us -> none  [shards(): piece = lax.all_gather(cells, 'line', axis=1, tiled=True)]
    all_to_all x0 -> x1, starting transfers between devices: none -> 6.72 us  [shards(): lax.all_to_all(jnp.stack([cells] * lax.axis_size('line')), 'line', 0, 0)]
  transfers between devices with their start and end apart: 3 -> 3, of which waited for: 2 -> 2; matrix products, arithmetic and copies ran while one was open for 15% -> 14% of each run, Pallas kernels for 0% -> 0%
where the time goes in v1:
time: 422 us; the launch traced here: 415 us
  matrix products  145 us (34%)
  waiting for transfers between devices  129 us (31%)
  local copies, waits for them, and re-layouts  66.9 us (16%)
  blocking collectives  35 us (8%)
  between operations  16.5 us (4%)
  starting transfers between devices  13.9 us (3%)
  other arithmetic  9.13 us (2%)
    dot_general x25, matrix products, contract(): jnp.einsum(form, left_op, right_op, preferred_element_type=jnp.float32)  145 us
    reduce_scatter x1, waiting for transfers between devices, shards(): lax.psum_scatter(partial_image, 'line', scatter_dimension=1, tiled=True)  93.7 us
    all_to_all x1, blocking collectives, shards(): lax.all_to_all(jnp.stack([plan_re, plan_im], axis=1), 'slab', split_axis=...  35 us
    all_to_all x1, waiting for transfers between devices, shards(): lax.all_to_all(jnp.stack([cells] * lax.axis_size('line')), 'line', 0, 0)  34.9 us
    slice x1, local copies, waits for them, and re-layouts, shards(): overwritten_result[:, 0]  12.3 us
    squeeze x1, local copies, waits for them, and re-layouts, shards(): overwritten_result[:, 0]  10.7 us
    squeeze x1, local copies, waits for them, and re-layouts, shards(): overwritten_result[:, 1]  10.6 us
    sub x1, local copies, waits for them, and re-layouts, shards(): partial_image + contract('ky,zkx->zxy', plane_cos, returned[1, 0])  10.3 us
  transfers between devices with their start and end apart: 3, of which 2 were waited for; matrix products, arithmetic and copies ran while one was open for 14% of the time, Pallas kernels for 0%

profile of v1, /device:TPU:0, one launch (start us, length us, event | category | flops | bytes accessed | tf_op | source)
XLA Modules:
  0.0 415.0 jit_solution(16227959412307347791)
XLA Ops:
  6.5 1.1 convert_element_type.109
  7.6 2.4 stack.64
  10.0 6.7 %all-to-all-start = ((bf16[16,32,16,256]{3,2,1,0:T(8,128)(2,1)}), bf16[16,32,16,256]{3,2,1,0:T(8,128)(2,1)}, u32[]{:S(2)}, u32[]{:S(2)}) async-start(bf16[16,32,16,256]{3,2,1,0:T(8,128)(2,1)} %stack.64), calls=%async_computation | async-start | bytes 8388608 | tf_op jit(solution)/shard_map/all_to_all | solution.py:45
  16.8 0.6 fusion.223
  19.9 0.0 copy-done
  19.9 0.2 copy.71
  20.1 12.0 %convolution_bitcast_fusion = f32[2,2,512,4,4,128]{5,4,3,1,2,0:T(4,128)} fusion(bf16[2,2,512,4,2,128]{5,4,3,2,1,0:T(2,128)(2,1)} %param.9, s32[512,2,2]{2,0,1:T(8,128)S(1)} %copy.71), kind=kOutput, calls=%fused_computation | convolution fusion | flops 16785408 | bytes 20979712 | tf_op jit(solution)/shard_map/voef,ozvnei->ozvnfi/dot_general | solution.py:21
  32.2 34.9 %all-to-all-done = bf16[16,32,16,256]{3,2,1,0:T(8,128)(2,1)} async-done(((bf16[16,32,16,256]{3,2,1,0:T(8,128)(2,1)}), bf16[16,32,16,256]{3,2,1,0:T(8,128)(2,1)}, u32[]{:S(2)}, u32[]{:S(2)}) %all-to-all-start) | async-done | bytes 4194336 | tf_op jit(solution)/shard_map/all_to_all | solution.py:45
  67.1 2.7 copy.73
  69.8 1.0 fusion.43
  70.8 1.0 fusion.40
  71.8 1.4 fusion.42
  73.2 1.4 fusion.41
  74.6 0.2 maximum_bitcast_fusion
  74.8 0.2 pad_maximum_fusion
  75.0 2.5 copy.74
  77.5 6.6 %all-to-all-start.1 = ((bf16[2,2,32,32,256]{4,2,1,0,3:T(8,128)(2,1)}), bf16[2,2,32,32,256]{4,2,1,0,3:T(8,128)(2,1)S(1)}, u32[]{:S(2)}, u32[]{:S(2)}) async-start(bf16[2,2,32,32,256]{4,2,1,0,3:T(8,128)(2,1)} %copy.74), calls=%async_computation.1 | async-start | bytes 4194304 | tf_op jit(solution)/shard_map/all_to_all | solution.py:56
  84.2 0.5 reduce-scatter.2.cloned.1.call-start
  84.7 12.3 %fusion.222 = (f32[2,1,512,4,4,128]{5,4,3,1,2,0:T(4,128)}, f32[2,1,512,4,4,128]{5,4,3,1,2,0:T(4,128)}) fusion(f32[2,2,512,4,4,128]{5,4,3,1,2,0:T(4,128)} %convolution_bitcast_fusion), kind=kLoop, calls=%fused_computation.250 | loop fusion | bytes 33554432 | tf_op jit(solution)/shard_map/slice | solution.py:99
  96.9 10.6 %squeeze.33 = f32[2,512,4,512]{3,2,1,0:T(4,128)} reshape(f32[2,1,512,4,4,128]{5,4,3,1,2,0:T(4,128)} %get-tuple-element.6) | data formatting | bytes 16777216 | tf_op jit(solution)/shard_map/squeeze | solution.py:104
  107.6 5.8 %fusion.56 = pred[512,2,4]{2,0,1:T(8,128)(4,1)S(1)} fusion(s32[512,2,2]{2,0,1:T(8,128)S(1)} %copy.71), kind=kLoop, calls=%fused_computation.68 | loop fusion | flops 12288 | bytes 12288 | tf_op jit(solution)/shard_map/reduce_or | solution.py:85
  113.4 3.5 and.95
  116.9 0.5 and.96
  117.4 10.7 %squeeze.30 = f32[2,512,4,512]{3,2,1,0:T(4,128)} reshape(f32[2,1,512,4,4,128]{5,4,3,1,2,0:T(4,128)} %get-tuple-element.5) | data formatting | bytes 16777216 | tf_op jit(solution)/shard_map/squeeze | solution.py:99
  128.1 0.1 broadcast_multiply_fusion
  128.1 0.3 broadcast_and_fusion
  128.4 0.0 all-to-all-done.1
  128.4 0.2 copy.76
  128.6 2.7 fusion.58
  131.3 2.7 fusion.57
  133.9 3.1 fusion.25
  137.0 3.3 fusion.24
  140.3 0.0 slice-start
  140.3 11.8 %fusion.18 = f32[4,2,512,512]{3,2,1,0:T(8,128)} fusion(bf16[2,512,4,256]{1,3,2,0:T(8,128)(2,1)S(1)} %fusion.25, s32[256]{0:T(256)S(1)} %iota_add_fusion.1, s32[4,512]{1,0:T(4,128)S(1)} %broadcast_multiply_fusion), kind=kOutput, calls=%fused_computation.37 | convolution fusion | flops 1082130432 | bytes 10494976 | tf_op jit(solution)/shard_map/klc,gakc->gakl/dot_general | solution.py:21
  152.2 8.9 %fusion.22 = f32[4,2,512,512]{3,2,1,0:T(8,128)S(1)} fusion(bf16[2,512,4,256]{1,3,2,0:T(8,128)(2,1)S(1)} %fusion.24, s32[256]{0:T(256)S(1)} %iota_add_fusion.1, s32[4,512]{1,0:T(4,128)S(1)} %broadcast_multiply_fusion), kind=kOutput, calls=%fused_computation.41 | convolution fusion | flops 1082130432 | bytes 10494976 | tf_op jit(solution)/shard_map/klc,gakc->gakl/dot_general | solution.py:21
  161.1 0.0 slice-done
  161.1 0.0 slice-done.1
  161.1 0.0 slice-start.3
  161.1 15.3 %fusion.2 = bf16[2,512,4,512]{3,1,0,2:T(8,128)(2,1)} fusion(f32[2,512,4,512]{3,2,1,0:T(4,128)S(1)} %bitcast.162, f32[4,2,512,512]{3,2,1,0:T(8,128)} %fusion.18, f32[4]{0:T(128)S(1)} %add_multiply_fusion, pred[2,512,512]{2,1,0:T(8,128)(4,1)S(1)} %broadcast_and_fusion, bf16[2,512,4,256]{1,3,2,0:T(8,128)(2,1)S(1)} %fusion.24, s32[256]{0:T(256)S(1)} %iota_add_fusion.1, ...), kind=kOutput, calls=%fused_computation.5 | convolution fusion | flops 1090519040 | bytes 23602192 | tf_op jit(solution)/shard_map/klc,gakc->gakl/dot_general | solution.py:21
  176.4 12.2 %fusion.50 = f32[4,2,512,256]{3,2,1,0:T(8,128)} fusion(bf16[2,512,4,512]{3,1,0,2:T(8,128)(2,1)} %fusion.2, s32[256]{0:T(256)S(1)} %iota_add_fusion.1, s32[4,512]{1,0:T(4,128)S(1)} %broadcast_multiply_fusion), kind=kOutput, calls=%fused_computation.65 | convolution fusion | flops 1082130432 | bytes 8397824 | tf_op jit(solution)/shard_map/klc,gakl->gakc/dot_general | solution.py:21
  188.7 0.0 slice-done.2
  188.7 12.5 %fusion.4 = bf16[2,512,4,512]{3,1,0,2:T(8,128)(2,1)S(1)} fusion(f32[2,512,4,512]{3,2,1,0:T(4,128)S(1)} %bitcast.164, f32[4,2,512,512]{3,2,1,0:T(8,128)S(1)} %fusion.22, f32[4]{0:T(128)S(1)} %add_multiply_fusion, pred[2,512,512]{2,1,0:T(8,128)(4,1)S(1)} %broadcast_and_fusion, bf16[2,512,4,256]{1,3,2,0:T(8,128)(2,1)S(1)} %fusion.25, ...), kind=kOutput, calls=%fused_computation.8 | convolution fusion | flops 1090519040 | bytes 23602192 | tf_op jit(solution)/shard_map/klc,gakc->gakl/dot_general | solution.py:21
  201.2 8.5 %fusion.53 = f32[4,2,512,256]{3,2,1,0:T(8,128)S(1)} fusion(bf16[2,512,4,512]{3,1,0,2:T(8,128)(2,1)S(1)} %fusion.4, s32[256]{0:T(256)S(1)} %iota_add_fusion.1, s32[4,512]{1,0:T(4,128)S(1)} %broadcast_multiply_fusion), kind=kOutput, calls=%fused_computation.66 | convolution fusion | flops 1082130432 | bytes 8397824 | tf_op jit(solution)/shard_map/klc,gakl->gakc/dot_general | solution.py:21
  209.7 9.8 %fusion.27 = bf16[2,512,4,256]{3,1,0,2:T(8,128)(2,1)S(1)} fusion(f32[4,2,512,256]{3,2,1,0:T(8,128)S(1)} %copy-done.5, bf16[2,512,4,512]{3,1,0,2:T(8,128)(2,1)S(1)} %fusion.4, s32[256]{0:T(256)S(1)} %iota_add_fusion.1, s32[4,512]{1,0:T(4,128)S(1)} %broadcast_multiply_fusion), kind=kOutput, calls=%fused_computation.46 | convolution fusion | flops 1084227584 | bytes 10494976 | tf_op jit(solution)/shard_map/klc,gakl->gakc/dot_general | solution.py:21
  219.6 2.7 fusion.10
  222.3 2.7 fusion.12
  225.0 9.9 %fusion.26 = bf16[2,512,4,256]{3,1,0,2:T(8,128)(2,1)S(1)} fusion(f32[4,2,512,256]{3,2,1,0:T(8,128)S(1)} %fusion.53, bf16[2,512,4,512]{3,1,0,2:T(8,128)(2,1)S(1)} %copy-done.4, s32[256]{0:T(256)S(1)} %iota_add_fusion.1, s32[4,512]{1,0:T(4,128)S(1)} %broadcast_multiply_fusion), kind=kOutput, calls=%fused_computation.45 | convolution fusion | flops 1084227584 | bytes 10494976 | tf_op jit(solution)/shard_map/klc,gakl->gakc/dot_general | solution.py:21
  234.9 2.7 fusion.35
  237.6 2.7 fusion.32
  240.4 0.2 pad_maximum_fusion.1
  240.6 3.1 copy.89
  243.7 35.0 %all_to_all.41 = bf16[2,2,256,4,256]{4,3,0,1,2:T(4,128)(2,1)S(1)} all-to-all(bf16[2,2,256,4,256]{4,3,0,1,2:T(4,128)(2,1)} %copy.89), channel_id=1, replica_groups=mesh['slab'=8,'line'=16] {'slab'}, dimensions={2} | all-to-all | bytes 4194304 | tf_op jit(solution)/shard_map/all_to_all | solution.py:122
  278.7 0.7 copy.90
  279.4 3.0 copy.91
  282.4 2.5 all_to_all.37
  285.0 1.5 fusion.62
  286.5 1.4 fusion.64
  287.9 4.7 %fusion.63 = f32[32,256,256]{2,1,0:T(8,128)} fusion(bf16[2,2,32,32,256]{4,3,2,1,0:T(8,128)(2,1)S(1)} %all_to_all.37, s32[256]{0:T(256)S(1)} %iota_add_fusion.1, s32[32]{0:T(128)S(1)} %fusion.98), kind=kOutput, calls=%fused_computation.84 | convolution fusion | flops 134348800 | bytes 8914432 | tf_op jit(solution)/shard_map/kx,zky->zxy/dot_general | solution.py:21
  292.6 8.9 %fusion = f32[32,256,256]{1,2,0:T(8,128)} fusion(f32[32,256,256]{1,2,0:T(8,128)S(1)} %fusion.62, f32[32,256,256]{2,1,0:T(8,128)S(1)} %fusion.64, f32[32,256,256]{2,1,0:T(8,128)} %fusion.63, bf16[2,2,32,32,256]{4,3,2,1,0:T(8,128)(2,1)S(1)} %all_to_all.37, s32[256]{0:T(256)S(1)} %iota_add_fusion.1, s32[32]{0:T(128)S(1)} %fusion.98), kind=kOutput, calls=%fused_computation.2 | convolution fusion | flops 140640256 | bytes 34080256 | tf_op jit(solution)/shard_map/ky,zkx->zxy/dot_general | solution.py:21
  301.5 10.3 %copy.94 = f32[32,256,256]{2,0,1:T(8,128)} copy(f32[32,256,256]{1,2,0:T(8,128)} %fusion) | data formatting | bytes 16777216 | tf_op jit(solution)/shard_map/sub | solution.py:129
  311.8 0.0 reduce-scatter.2.cloned.1.call-update
  311.8 93.7 %reduce-scatter.2.cloned.1.call-done = f32[32,16,256]{2,0,1:T(8,128)} async-done(((f32[32,256,256]{2,0,1:T(8,128)}), f32[32,16,256]{2,0,1:T(8,128)}) %reduce-scatter.2.cloned.1.call-update) | async-done | bytes 524304 | tf_op jit(solution)/shard_map/reduce_scatter | solution.py:133
  405.5 1.2 fusion.68
  406.7 1.1 copy.95
  (22 shorter events, 0.1 us)
Async XLA Ops:
  10.0 6.7 %copy-start.3 = (s32[2]{0:T(128)S(1)}, s32[2]{0:T(128)}, u32[]{:S(2)}) copy-start(s32[2]{0:T(128)} %param.11) | copy-start | bytes 28
  10.0 9.9 %copy-start = (s32[512,2,2]{0,2,1:T(2,128)S(1)}, s32[512,2,2]{0,2,1:T(2,128)}, u32[]{:S(2)}) copy-start(s32[512,2,2]{0,2,1:T(2,128)} %param.10) | copy-start | bytes 24580
  10.0 57.1 %all-to-all-start = ((bf16[16,32,16,256]{3,2,1,0:T(8,128)(2,1)}), bf16[16,32,16,256]{3,2,1,0:T(8,128)(2,1)}, u32[]{:S(2)}, u32[]{:S(2)}) async-start(bf16[16,32,16,256]{3,2,1,0:T(8,128)(2,1)} %stack.64), calls=%async_computation | async-start | bytes 8388608 | tf_op jit(solution)/shard_map/all_to_all | solution.py:45
  77.5 50.9 %all-to-all-start.1 = ((bf16[2,2,32,32,256]{4,2,1,0,3:T(8,128)(2,1)}), bf16[2,2,32,32,256]{4,2,1,0,3:T(8,128)(2,1)S(1)}, u32[]{:S(2)}, u32[]{:S(2)}) async-start(bf16[2,2,32,32,256]{4,2,1,0,3:T(8,128)(2,1)} %copy.74), calls=%async_computation.1 | async-start | bytes 4194304 | tf_op jit(solution)/shard_map/all_to_all | solution.py:56
  84.2 321.3 %reduce-scatter.2.cloned.1.call-start = ((), (), s32[]{:S(2)}) async-start(), calls=%async_computation.4 | async-start | bytes 8912896 | tf_op jit(solution)/shard_map/reduce_scatter | solution.py:133
  140.3 20.7 %slice-start = ((s8[8388608]{0:T(1024)(128)(4,1)}), s8[4194304]{0:T(1024)(128)(4,1)S(1)}, s32[]{:S(2)}) async-start(s8[8388608]{0:T(1024)(128)(4,1)} %bitcast.161), calls=%async_computation.5 | async-start | bytes 8388608
  152.2 8.9 %slice-start.1 = ((s8[8388608]{0:T(1024)(128)(4,1)}), s8[4194304]{0:T(1024)(128)(4,1)S(1)}, s32[]{:S(2)}) async-start(s8[8388608]{0:T(1024)(128)(4,1)} %bitcast.161), calls=%async_computation.6 | async-start | bytes 8388608
  152.2 36.5 %slice-start.2 = ((s8[8388608]{0:T(1024)(128)(4,1)}), s8[4194304]{0:T(1024)(128)(4,1)S(1)}, s32[]{:S(2)}) async-start(s8[8388608]{0:T(1024)(128)(4,1)} %bitcast.163), calls=%async_computation.7 | async-start | bytes 8388608
  161.1 27.6 %slice-start.3 = ((s8[8388608]{0:T(1024)(128)(4,1)}), s8[4194304]{0:T(1024)(128)(4,1)S(1)}, s32[]{:S(2)}) async-start(s8[8388608]{0:T(1024)(128)(4,1)} %bitcast.163), calls=%async_computation.8 | async-start | bytes 8388608
  201.2 8.5 %copy-start.5 = (f32[4,2,512,256]{3,2,1,0:T(8,128)S(1)}, f32[4,2,512,256]{3,2,1,0:T(8,128)}, u32[]{:S(2)}) copy-start(f32[4,2,512,256]{3,2,1,0:T(8,128)} %fusion.50) | copy-start | bytes 12582916
  222.3 2.7 copy-start.4
  311.8 93.7 %copy-start.1 = (s32[32,16]{0,1:T(8,128)S(1)}, s32[32,16]{0,1:T(8,128)}, u32[]{:S(2)}) copy-start(s32[32,16]{0,1:T(8,128)} %param.8) | copy-start | bytes 6148
  311.8 93.7 %copy-start.2 = (s32[32,16]{0,1:T(8,128)S(1)}, s32[32,16]{0,1:T(8,128)}, u32[]{:S(2)}) copy-start(s32[32,16]{0,1:T(8,128)} %param.7) | copy-start | bytes 6148
Sparse Core Ops, SparseCore 0:
  311.9 93.5 reduce-scatter.1
